TPU v7x, 32 devices: a whole 2x2x4 slice. The times are simulated.
32 devices in a mesh: batch: 4 (over x, core), hidden: 4 (over z), solver: 2 (over y).
Axes of the slice: x: 2, y: 2, z: 4, core: 2. Of those that a mesh axis runs over, the one named last changes fastest.
Arguments:
- activations: bfloat16 [1024, 4096], P('batch', ('hidden', 'solver')), may hold values from -16 to 16, as said below
- cotangent: bfloat16 [8192, 1024], P(('hidden', 'solver'), 'batch'), may hold values from -0.1875 to 0.1875
- weight: bfloat16 [4096, 8192], P(('hidden', 'solver'), 'batch'), may hold values from -0.09375 to 0.09375
- left_old: float32 [4, 8, 1024, 1024], P('hidden', 'batch'), may hold values from -0.001953125 to 2.0019531, as said below
- right_old: float32 [4, 8, 1024, 1024], P('hidden', 'batch'), may hold values from -0.001953125 to 2.0019531, as said below
Outputs:
- first_out: bfloat16 [8192, 1024], P(('hidden', 'solver'), 'batch')
- new_left: float32 [4, 8, 1024, 1024], P('hidden', 'batch', 'solver')
- new_right: float32 [4, 8, 1024, 1024], P('hidden', 'batch', 'solver')
- direction: float32 [4096, 8192], P(('hidden', 'solver'), 'batch')
- second_out: bfloat16 [8192, 1024], P(('hidden', 'solver'), 'batch')
Inputs may be any that keep to these rules, and one draw needn't show every extreme that they name: `activations`: in the hidden draw each feature carries its own scale. `left_old`: every block is symmetric, its diagonal is positive and larger than the sum of the magnitudes of the rest of its row. `right_old`: every block is symmetric, its diagonal is positive and larger than the sum of the magnitudes of the rest of its row.
All inputs are finite; a program needn't handle non-finite values. Where the computation divides by a largest or mean magnitude, that divisor is 1e-20 or more.
Results may differ from a plain program's by a relative error of at most 0.017.
Values may be sent and summed in bfloat16 or wider, within the bound.
A program may use at most 128 MiB of HBM per device.

v0:
```python
import jax
import jax.numpy as jnp
from jax import lax
from jax.sharding import PartitionSpec as P

BLOCK = 1024
STAT_DECAY = 0.8
LEARN_RATE = 0.005
EPSILON = 1e-06


def product(left_mat, right_mat):
    return jnp.einsum(
        "bij,bjk->bik",
        left_mat,
        right_mat,
        precision=lax.Precision.HIGHEST,
        preferred_element_type=jnp.float32,
    )


def prepare(factor):
    identity = jnp.eye(BLOCK, dtype=jnp.float32)
    scaled = 2.5 / (jnp.max(jnp.sum(jnp.abs(factor), axis=2), axis=1) + EPSILON)
    moment = scaled[:, None, None] * factor
    newton_step = (5.0 * identity - moment) * 0.25
    return (scaled, moment, newton_step)


def transposed_product(weight_cols, acts):
    return lax.dot_general(
        weight_cols, acts, (((0,), (1,)), ((), ())), preferred_element_type=jnp.float32
    )


def body(activations, cotangent, weight, left_old, right_old):
    rows_here = weight.shape[0]
    nblocks = weight.shape[1] // BLOCK
    weight_rows = lax.all_gather(weight, "batch", axis=1, tiled=True)
    columns = weight_rows
    first_sum = lax.psum_scatter(
        transposed_product(columns, activations).astype(jnp.bfloat16),
        ("hidden", "solver"),
        scatter_dimension=0,
        tiled=True,
    )
    cotangent_all = lax.all_gather(cotangent, ("hidden", "solver"), axis=0, tiled=True)
    grad_local = lax.psum_scatter(
        jnp.dot(cotangent_all, activations, preferred_element_type=jnp.float32).astype(
            jnp.bfloat16
        ),
        "batch",
        scatter_dimension=0,
        tiled=True,
    )
    grad_blocks = grad_local.reshape(nblocks, BLOCK, rows_here)
    grad_full = lax.all_gather(grad_blocks, "solver", axis=2, tiled=True)
    gram_left = jnp.einsum("bnm,bnk->bmk", grad_full, grad_full, preferred_element_type=jnp.float32)
    gram_right = jnp.einsum(
        "bnm,bkm->bnk", grad_full, grad_full, preferred_element_type=jnp.float32
    )
    left_all = STAT_DECAY * left_old[0] + (1.0 - STAT_DECAY) / BLOCK * gram_left
    right_all = STAT_DECAY * right_old[0] + (1.0 - STAT_DECAY) / BLOCK * gram_right
    first_row = lax.axis_index("solver") * rows_here
    new_left = lax.dynamic_slice_in_dim(left_all, first_row, rows_here, 1)[None]
    new_right = lax.dynamic_slice_in_dim(right_all, first_row, rows_here, 1)[None]
    scale_left, moment_left, step_left = prepare(left_all)
    own_rows = lax.dynamic_slice_in_dim(step_left, first_row, rows_here, 1)
    power_rows = product(
        product(product(product(own_rows, step_left), step_left), step_left), moment_left
    )
    row_index = lax.broadcasted_iota(jnp.int32, (rows_here, BLOCK), 0) + first_row
    col_index = lax.broadcasted_iota(jnp.int32, (rows_here, BLOCK), 1)
    eye_rows = (row_index == col_index).astype(jnp.float32)
    next_rows = (5.0 * eye_rows - power_rows) * 0.25
    root_rows = (scale_left**0.25)[:, None, None] * product(next_rows, step_left)
    grad_float = grad_full.astype(jnp.float32)
    mixed_rows = jnp.einsum(
        "brm,bnm->brn",
        root_rows,
        grad_float,
        precision=lax.Precision.HIGHEST,
        preferred_element_type=jnp.float32,
    )
    scale_right, moment_right, step_right = prepare(right_all)
    turned = product(mixed_rows, step_right)
    power_right = product(
        product(product(product(product(turned, step_right), step_right), step_right), step_right),
        moment_right,
    )
    update = (scale_right**0.25)[:, None, None] * ((5.0 * turned - power_right) * 0.25)
    squares = lax.psum(jnp.sum(update * update, axis=(1, 2)), "solver")
    spread = jnp.sqrt(squares / (BLOCK * BLOCK) + EPSILON)
    scaled_update = update / spread[:, None, None]
    direction = jnp.transpose(scaled_update, (1, 0, 2)).reshape(rows_here, nblocks * BLOCK)
    new_weight = (weight.astype(jnp.float32) - LEARN_RATE * direction).astype(jnp.bfloat16)
    new_rows = lax.all_gather(new_weight, "batch", axis=1, tiled=True)
    columns = new_rows
    second_sum = lax.psum_scatter(
        transposed_product(columns, activations).astype(jnp.bfloat16),
        ("hidden", "solver"),
        scatter_dimension=0,
        tiled=True,
    )
    return (first_sum, new_left, new_right, direction, second_sum)


def solution(mesh):
    in_specs = (
        P("batch", ("hidden", "solver")),
        P(("hidden", "solver"), "batch"),
        P(("hidden", "solver"), "batch"),
        P("hidden", "batch", None, None),
        P("hidden", "batch", None, None),
    )
    out_specs = (
        P(("hidden", "solver"), "batch"),
        P("hidden", "batch", "solver", None),
        P("hidden", "batch", "solver", None),
        P(("hidden", "solver"), "batch"),
        P(("hidden", "solver"), "batch"),
    )
    return jax.shard_map(body, mesh=mesh, in_specs=in_specs, out_specs=out_specs, check_vma=False)
```

profile of v0, /device:TPU:0, one launch (start us, length us, event | category | flops | bytes accessed | tf_op | source)
XLA Modules:
  0.0 721.3 jit_solution(6583412201741329409)
XLA Ops:
  7.2 0.7 all-gather.7.cloned.1.call-update
  8.0 77.7 %all-gather.7.cloned.1.call-done = bf16[8192,256]{1,0:T(8,128)(2,1)} async-done(((bf16[1024,256]{1,0:T(8,128)(2,1)}), bf16[8192,256]{1,0:T(8,128)(2,1)}) %all-gather.7.cloned.1.call-update) | async-done | bytes 4194320 | tf_op jit(solution)/shard_map/all_gather | solution.py:47
  85.7 7.8 %convolution_convert_fusion = bf16[8192,512]{1,0:T(8,128)(2,1)} fusion(bf16[8192,256]{1,0:T(8,128)(2,1)} %all-gather.7.cloned.1.call-done, bf16[256,512]{1,0:T(8,128)(2,1)S(1)} %copy-done), kind=kOutput, calls=%fused_computation | convolution fusion | flops 2151677952 | bytes 12845056 | tf_op jit(solution)/shard_map/dot_general | solution.py:49
  93.5 0.0 all-gather.9.cloned.1.call-start
  93.5 70.0 %reduce-scatter.6.cloned.1.call-done = bf16[2048,512]{1,0:T(8,128)(2,1)} async-done(((bf16[8192,512]{1,0:T(8,128)(2,1)}), bf16[2048,512]{1,0:T(8,128)(2,1)}) %reduce-scatter.6.cloned.1.call-update) | async-done | bytes 2097168 | tf_op jit(solution)/shard_map/reduce_scatter | solution.py:48
  163.5 3.9 copy.32
  167.5 0.0 all-gather.5.cloned.1.call-start
  167.5 0.5 all-gather.5.cloned.1.call-update
  168.0 0.2 all-gather.11.cloned.1.call-start
  168.3 2.5 fusion.13
  170.8 2.5 copy.53
  173.3 9.1 %copy.31 = f32[1,2,1024,1024]{2,3,1,0:T(8,128)} copy(f32[1,2,1024,1024]{3,2,1,0:T(8,128)} %param.8) | data formatting | bytes 16777216 | tf_op args[3]
  182.4 8.7 %copy.35 = f32[1,2,1024,1024]{2,3,1,0:T(8,128)} copy(f32[1,2,1024,1024]{3,2,1,0:T(8,128)} %param.9) | data formatting | bytes 16777216 | tf_op args[4]
  191.1 0.2 fusion.17
  191.3 33.1 %all-gather.9.cloned.1.call-done = bf16[2,1024,1024]{1,2,0:T(8,128)(2,1)} async-done(((bf16[2,1024,512]{1,2,0:T(8,128)(2,1)}), bf16[2,1024,1024]{1,2,0:T(8,128)(2,1)}) %all-gather.9.cloned.1.call-update) | async-done | bytes 4194320 | tf_op jit(solution)/shard_map/all_gather | solution.py:57
  224.4 15.2 %abs_reduce_fusion.1 = (f32[2,1024]{1,0:T(2,128)S(1)}, f32[2,1024,1024]{1,2,0:T(8,128)}) fusion(bf16[2,1024,1024]{1,2,0:T(8,128)(2,1)} %all-gather.9.cloned.1.call-done, f32[1,2,1024,1024]{2,3,1,0:T(8,128)} %copy.31), kind=kOutput, calls=%fused_computation.8 | convolution fusion | flops 4305451008 | bytes 20979712 | tf_op jit(solution)/shard_map/bnm,bnk->bmk/dot_general | solution.py:58
  239.6 10.1 %abs_reduce_fusion = (f32[2,1024]{1,0:T(2,128)S(1)}, f32[2,1024,1024]{1,2,0:T(8,128)}) fusion(bf16[2,1024,1024]{1,2,0:T(8,128)(2,1)S(1)} %copy-done.4, f32[1,2,1024,1024]{2,3,1,0:T(8,128)} %copy.35), kind=kOutput, calls=%fused_computation.6 | convolution fusion | flops 4305451008 | bytes 20979712 | tf_op jit(solution)/shard_map/bnm,bkm->bnk/dot_general | solution.py:59
  249.7 0.1 reduce_max.18
  249.8 0.1 reduce_max.19
  250.0 11.5 %subtract_multiply_fusion = (f32[2,1024,1024]{1,2,0:T(8,128)S(1)}, f32[2,1024,1024]{1,2,0:T(8,128)}) fusion(f32[2,1024,1024]{1,2,0:T(8,128)} %get-tuple-element.22, f32[2]{0:T(128)S(1)} %get-tuple-element.16, f32[1024,1024]{0,1:T(8,128)} %fusion.13, f32[2,1024,1024]{1,2,0:T(8,128)} %get-tuple-element.24, f32[2]{0:T(128)S(1)} %get-tuple-element.28), kind=kLoop, calls=%fused_computation.5 | loop fusion | flops 12582912 | bytes 37748752 | tf_op jit(solution)/shard_map/mul | solution.py:26
  261.4 31.4 %fusion.10 = f32[2,512,1024]{2,1,0:T(8,128)S(1)} fusion(f32[2,1024,1024]{1,2,0:T(8,128)} %get-tuple-element.20, s32[]{:T(128)S(6)} %select_n.2), kind=kOutput, calls=%fused_computation.23 | convolution fusion | flops 12884901888 | bytes 16777220 | tf_op jit(solution)/shard_map/bij,bjk->bik/dot_general | solution.py:13
  292.9 14.3 %fusion.22 = f32[2,512,1024]{2,1,0:T(8,128)S(1)} fusion(f32[2,512,1024]{2,1,0:T(8,128)S(1)} %fusion.10, f32[2,1024,1024]{1,2,0:T(8,128)S(1)} %copy-done.1), kind=kOutput, calls=%fused_computation.43 | convolution fusion | flops 12884901888 | bytes 16777216 | tf_op jit(solution)/shard_map/bij,bjk->bik/dot_general | solution.py:13
  307.1 14.3 %fusion.23 = f32[2,512,1024]{2,1,0:T(8,128)S(1)} fusion(f32[2,512,1024]{2,1,0:T(8,128)S(1)} %fusion.22, f32[2,1024,1024]{1,2,0:T(8,128)S(1)} %copy-done.1), kind=kOutput, calls=%fused_computation.44 | convolution fusion | flops 12884901888 | bytes 16777216 | tf_op jit(solution)/shard_map/bij,bjk->bik/dot_general | solution.py:13
  321.5 16.3 %fusion.2 = f32[2,512,1024]{2,1,0:T(8,128)S(1)} fusion(f32[2,512,1024]{2,1,0:T(8,128)S(1)} %fusion.23, f32[2,1024,1024]{1,2,0:T(8,128)} %get-tuple-element.24, f32[2]{0:T(128)S(1)} %get-tuple-element.28), kind=kOutput, calls=%fused_computation.11 | convolution fusion | flops 12886999040 | bytes 16777224 | tf_op jit(solution)/shard_map/bij,bjk->bik/dot_general | solution.py:13
  337.8 15.6 %fusion.7 = f32[2,512,1024]{2,1,0:T(8,128)} fusion(f32[2,1024,1024]{1,2,0:T(8,128)S(1)} %copy-done.1, f32[2,512,1024]{2,1,0:T(8,128)S(1)} %fusion.2, f32[512,1024]{1,0:T(8,128)S(1)} %fusion.17), kind=kOutput, calls=%fused_computation.20 | convolution fusion | flops 12886999040 | bytes 18874368 | tf_op jit(solution)/shard_map/bij,bjk->bik/dot_general | solution.py:13
  353.4 9.4 %fusion.5 = f32[2,512,1024]{2,1,0:T(8,128)S(1)} fusion(bf16[2,1024,1024]{1,2,0:T(8,128)(2,1)} %all-gather.9.cloned.1.call-done, f32[2,512,1024]{2,1,0:T(8,128)} %fusion.7, f32[2]{0:T(128)S(1)} %get-tuple-element.27), kind=kOutput, calls=%fused_computation.18 | convolution fusion | flops 12885950464 | bytes 12582920 | tf_op jit(solution)/shard_map/brm,bnm->brn/dot_general | solution.py:78
  362.8 14.3 %fusion.24 = f32[2,512,1024]{2,1,0:T(8,128)S(1)} fusion(f32[2,512,1024]{2,1,0:T(8,128)S(1)} %fusion.5, f32[2,1024,1024]{1,2,0:T(8,128)S(1)} %get-tuple-element.19), kind=kOutput, calls=%fused_computation.45 | convolution fusion | flops 12884901888 | bytes 16777216 | tf_op jit(solution)/shard_map/bij,bjk->bik/dot_general | solution.py:13
  377.2 14.6 %fusion.25 = f32[2,512,1024]{2,1,0:T(8,128)S(1)} fusion(f32[2,512,1024]{2,1,0:T(8,128)S(1)} %fusion.24, f32[2,1024,1024]{1,2,0:T(8,128)S(1)} %get-tuple-element.19), kind=kOutput, calls=%fused_computation.46 | convolution fusion | flops 12884901888 | bytes 16777216 | tf_op jit(solution)/shard_map/bij,bjk->bik/dot_general | solution.py:13
  391.7 14.3 %fusion.26 = f32[2,512,1024]{2,1,0:T(8,128)S(1)} fusion(f32[2,512,1024]{2,1,0:T(8,128)S(1)} %fusion.25, f32[2,1024,1024]{1,2,0:T(8,128)S(1)} %get-tuple-element.19), kind=kOutput, calls=%fused_computation.47 | convolution fusion | flops 12884901888 | bytes 16777216 | tf_op jit(solution)/shard_map/bij,bjk->bik/dot_general | solution.py:13
  406.0 14.4 %fusion.27 = f32[2,512,1024]{2,1,0:T(8,128)S(1)} fusion(f32[2,512,1024]{2,1,0:T(8,128)S(1)} %fusion.26, f32[2,1024,1024]{1,2,0:T(8,128)S(1)} %get-tuple-element.19), kind=kOutput, calls=%fused_computation.48 | convolution fusion | flops 12884901888 | bytes 16777216 | tf_op jit(solution)/shard_map/bij,bjk->bik/dot_general | solution.py:13
  420.4 14.7 %fusion.28 = f32[2,512,1024]{2,1,0:T(8,128)S(1)} fusion(f32[2,512,1024]{2,1,0:T(8,128)S(1)} %fusion.27, f32[2,1024,1024]{1,2,0:T(8,128)S(1)} %get-tuple-element.19), kind=kOutput, calls=%fused_computation.49 | convolution fusion | flops 12884901888 | bytes 16777216 | tf_op jit(solution)/shard_map/bij,bjk->bik/dot_general | solution.py:13
  435.2 16.0 %multiply_reduce_fusion = (f32[2]{0:T(128)S(1)}, f32[2,512,1024]{2,1,0:T(8,128)}) fusion(f32[2]{0:T(128)S(1)} %get-tuple-element.15, f32[2,512,1024]{2,1,0:T(8,128)S(1)} %fusion.28, f32[2,1024,1024]{1,2,0:T(8,128)S(1)} %bitcast.41, f32[2]{0:T(128)S(1)} %get-tuple-element.16, f32[2,512,1024]{2,1,0:T(8,128)S(1)} %fusion.24), kind=kOutput, calls=%fused_computation.15 | convolution fusion | flops 12892241920 | bytes 20971544 | tf_op jit(solution)/shard_map/bij,bjk->bik/dot_general | solution.py:13
  451.2 4.9 psum.7
  456.1 5.1 divide_bitcast_fusion
  461.2 5.5 copy.52
  466.7 4.2 subtract_convert_fusion
  471.0 0.0 reduce-scatter.4.cloned.1.call-start
  471.0 7.9 %convolution_convert_fusion.2 = bf16[8192,256]{1,0:T(8,128)(2,1)} fusion(bf16[512,8192]{1,0:T(8,128)(2,1)} %all-gather.5.cloned.1.call-done, bf16[256,512]{1,0:T(8,128)(2,1)S(1)} %copy-done), kind=kOutput, calls=%fused_computation.2 | convolution fusion | flops 2149580800 | bytes 12845056 | tf_op jit(solution)/shard_map/dot_general | solution.py:31
  478.9 0.3 reduce-scatter.8.cloned.1.call-start
  479.2 50.5 %all-gather.11.cloned.1.call-done = bf16[512,8192]{0,1:T(8,128)(2,1)} async-done(((bf16[512,2048]{0,1:T(8,128)(2,1)}), bf16[512,8192]{0,1:T(8,128)(2,1)}) %all-gather.11.cloned.1.call-update) | async-done | bytes 8388624 | tf_op jit(solution)/shard_map/all_gather | solution.py:97
  529.7 7.7 %convolution_convert_fusion.1 = bf16[8192,256]{1,0:T(8,128)(2,1)} fusion(bf16[512,8192]{0,1:T(8,128)(2,1)} %all-gather.11.cloned.1.call-done, bf16[256,512]{1,0:T(8,128)(2,1)S(1)} %copy-done), kind=kOutput, calls=%fused_computation.1 | convolution fusion | flops 2149580800 | bytes 12845056 | tf_op jit(solution)/shard_map/dot_general | solution.py:31
  537.4 5.4 copy.54
  542.8 4.6 constant_dynamic-slice_fusion.1
  547.4 5.4 copy.34
  552.8 4.6 constant_dynamic-slice_fusion
  557.5 5.5 copy.38
  562.9 59.1 %reduce-scatter.4.cloned.1.call-done = bf16[1024,256]{1,0:T(8,128)(2,1)} async-done(((bf16[8192,256]{1,0:T(8,128)(2,1)}), bf16[1024,256]{1,0:T(8,128)(2,1)}) %reduce-scatter.4.cloned.1.call-update) | async-done | bytes 524304 | tf_op jit(solution)/shard_map/reduce_scatter | solution.py:41
  622.1 92.1 %reduce-scatter.8.cloned.1.call-done = bf16[1024,256]{1,0:T(8,128)(2,1)} async-done(((bf16[8192,256]{1,0:T(8,128)(2,1)}), bf16[1024,256]{1,0:T(8,128)(2,1)}) %reduce-scatter.8.cloned.1.call-update) | async-done | bytes 524304 | tf_op jit(solution)/shard_map/reduce_scatter | solution.py:99
  (26 shorter events, 0.2 us)
Async XLA Ops:
  7.2 78.5 %copy-start = (bf16[256,512]{1,0:T(8,128)(2,1)S(1)}, bf16[256,512]{1,0:T(8,128)(2,1)}, u32[]{:S(2)}) copy-start(bf16[256,512]{1,0:T(8,128)(2,1)} %param.5) | copy-start | bytes 786436
  7.2 78.5 %all-gather.7.cloned.1.call-start = ((), (), s32[]{:S(2)}) async-start(), calls=%async_computation.5 | async-start | bytes 4718592 | tf_op jit(solution)/shard_map/all_gather | solution.py:47
  7.9 155.6 %reduce-scatter.6.cloned.1.call-start = ((), (), s32[]{:S(2)}) async-start(), calls=%async_computation.6 | async-start | bytes 10485760 | tf_op jit(solution)/shard_map/reduce_scatter | solution.py:48
  93.5 130.9 %all-gather.9.cloned.1.call-start = ((), (), s32[]{:S(2)}) async-start(), calls=%async_computation.7 | async-start | bytes 6291456 | tf_op jit(solution)/shard_map/all_gather | solution.py:57
  167.4 3.4 copy-start.2
  167.5 303.6 %all-gather.5.cloned.1.call-start = ((), (), s32[]{:S(2)}) async-start(), calls=%async_computation.3 | async-start | bytes 10485760 | tf_op jit(solution)/shard_map/all_gather | solution.py:39
  168.0 361.7 %all-gather.11.cloned.1.call-start = ((), (), s32[]{:S(2)}) async-start(), calls=%async_computation.8 | async-start | bytes 10485760 | tf_op jit(solution)/shard_map/all_gather | solution.py:97
  224.4 15.2 %copy-start.4 = (bf16[2,1024,1024]{1,2,0:T(8,128)(2,1)S(1)}, bf16[2,1024,1024]{1,2,0:T(8,128)(2,1)}, u32[]{:S(2)}) copy-start(bf16[2,1024,1024]{1,2,0:T(8,128)(2,1)} %all-gather.9.cloned.1.call-done) | copy-start | bytes 12582916
  261.4 31.5 %copy-start.1 = (f32[2,1024,1024]{1,2,0:T(8,128)S(1)}, f32[2,1024,1024]{1,2,0:T(8,128)}, u32[]{:S(2)}) copy-start(f32[2,1024,1024]{1,2,0:T(8,128)} %get-tuple-element.20) | copy-start | bytes 25165828
  406.0 29.1 %slice-start = ((s8[8388608]{0:T(1024)(128)(4,1)}), s8[4194304]{0:T(1024)(128)(4,1)S(1)}, s32[]{:S(2)}) async-start(s8[8388608]{0:T(1024)(128)(4,1)} %bitcast.40), calls=%async_computation.10 | async-start | bytes 8388608
  420.4 14.7 %slice-start.1 = ((s8[8388608]{0:T(1024)(128)(4,1)}), s8[4194304]{0:T(1024)(128)(4,1)S(1)}, s32[]{:S(2)}) async-start(s8[8388608]{0:T(1024)(128)(4,1)} %bitcast.40), calls=%async_computation.11 | async-start | bytes 8388608
  461.2 5.5 copy-start.3
  471.0 151.1 %reduce-scatter.4.cloned.1.call-start = ((), (), s32[]{:S(2)}) async-start(), calls=%async_computation.4 | async-start | bytes 4718592 | tf_op jit(solution)/shard_map/reduce_scatter | solution.py:41
  478.9 235.3 %reduce-scatter.8.cloned.1.call-start = ((), (), s32[]{:S(2)}) async-start(), calls=%async_computation.9 | async-start | bytes 4718592 | tf_op jit(solution)/shard_map/reduce_scatter | solution.py:99
Sparse Core Ops, SparseCore 0:
  10.1 75.5 all-gather.6
  93.6 69.8 reduce-scatter.5
  167.6 56.7 all-gather.8
  225.8 58.2 all-gather.4
  471.1 58.5 all-gather.10
  533.8 88.2 reduce-scatter.3
  626.3 87.8 reduce-scatter.7
where the time goes:
time: 725 us; the launch traced here: 721 us
  waiting for transfers between devices  384 us (53%)
  matrix products  238 us (33%)
  local copies, waits for them, and re-layouts  55.2 us (8%)
  other arithmetic  23.8 us (3%)
  between operations  14.5 us (2%)
    dot_general x11, matrix products, product(): jnp.einsum('bij,bjk->bik', left_mat, right_mat, precision=lax.Precision.H...  180 us
    reduce_scatter x2, waiting for transfers between devices, body(): lax.psum_scatter(transposed_product(columns, activations).astype(jnp.bflo...  151 us
    all_gather x1, waiting for transfers between devices, body(): lax.all_gather(cotangent, ('hidden', 'solver'), axis=0, tiled=True)  77.7 us
    reduce_scatter x1, waiting for transfers between devices, body(): lax.psum_scatter(jnp.dot(cotangent_all, activations, preferred_element_ty...  70 us
    all_gather x1, waiting for transfers between devices, body(): new_rows = lax.all_gather(new_weight, 'batch', axis=1, tiled=True)  50.5 us
    all_gather x1, waiting for transfers between devices, body(): grad_full = lax.all_gather(grad_blocks, 'solver', axis=2, tiled=True)  33.1 us
    unnamed x18, local copies, waits for them, and re-layouts  25.7 us
    dot_general x2, matrix products, transposed_product(): lax.dot_general(weight_cols, acts, (((0,), (1,)), ((), ())), preferred_el...  15.6 us
  transfers between devices with their start and end apart: 7, of which 6 were waited for; matrix products, arithmetic and copies ran while one was open for 42% of the time, Pallas kernels for 0%

commit v1 on v0

--- a/solution.py
+++ b/solution.py
@@ -1,3 +1,4 @@
+import functools
 import jax
 import jax.numpy as jnp
 from jax import lax
@@ -7,6 +8,22 @@
 STAT_DECAY = 0.8
 LEARN_RATE = 0.005
 EPSILON = 1e-06
+
+
+def _end_targets(local_values, chip_axis):
+    devs = lax.axis_size(chip_axis)
+    block_out = [(s - 1, s) for s in range(1, devs)] + [(devs - 1, 0)]
+    raw_out = local_values
+    items = [raw_out]
+    for _ in [*range(devs - 1)]:
+        raw_out = lax.ppermute(raw_out, axis_name=chip_axis, perm=block_out)
+        items += [raw_out]
+    after = jnp.concatenate([*reversed(items)], axis=1)
+    mat_out = jnp.roll(after, (lax.axis_index(chip_axis) + 1) * raw_out.shape[1], axis=1)
+    return mat_out
+
+
+fill_tables = functools.partial(_end_targets, chip_axis="batch")
 
 
 def product(left_mat, right_mat):
@@ -94,7 +111,7 @@
     scaled_update = update / spread[:, None, None]
     direction = jnp.transpose(scaled_update, (1, 0, 2)).reshape(rows_here, nblocks * BLOCK)
     new_weight = (weight.astype(jnp.float32) - LEARN_RATE * direction).astype(jnp.bfloat16)
-    new_rows = lax.all_gather(new_weight, "batch", axis=1, tiled=True)
+    new_rows = fill_tables(new_weight)
     columns = new_rows
     second_sum = lax.psum_scatter(
         transposed_product(columns, activations).astype(jnp.bfloat16),

time: 725 us -> 670 us (0.924)
  waiting for transfers between devices: 384 us -> 322 us
  local copies, waits for them, and re-layouts: 55.2 us -> 65.9 us
    reduce_scatter x2, waiting for transfers between devices: 151 us -> 71.1 us  [body(): lax.psum_scatter(transposed_product(columns, activations).astype(jnp.bflo...]
    ppermute x0 -> x3, waiting for transfers between devices: none -> 69.2 us  [_end_targets(): raw_out = lax.ppermute(raw_out, axis_name=chip_axis, perm=block_out)]
    all_gather x1 -> x0, waiting for transfers between devices: 50.5 us -> none  [body(): new_rows = lax.all_gather(new_weight, 'batch', axis=1, tiled=True)]
    unnamed x18 -> x23, local copies, waits for them, and re-layouts: 25.7 us -> 36.2 us
  transfers between devices with their start and end apart: 7 -> 9, of which waited for: 6 -> 7; matrix products, arithmetic and copies ran while one was open for 42% -> 47% of each run, Pallas kernels for 0% -> 0%
where the time goes in v1:
time: 670 us; the launch traced here: 666 us
  waiting for transfers between devices  322 us (48%)
  matrix products  235 us (35%)
  local copies, waits for them, and re-layouts  65.9 us (10%)
  other arithmetic  23.1 us (3%)
  between operations  14.6 us (2%)
    dot_general x11, matrix products, product(): jnp.einsum('bij,bjk->bik', left_mat, right_mat, precision=lax.Precision.H...  180 us
    all_gather x1, waiting for transfers between devices, body(): lax.all_gather(cotangent, ('hidden', 'solver'), axis=0, tiled=True)  77.7 us
    reduce_scatter x2, waiting for transfers between devices, body(): lax.psum_scatter(transposed_product(columns, activations).astype(jnp.bflo...  71.1 us
    reduce_scatter x1, waiting for transfers between devices, body(): lax.psum_scatter(jnp.dot(cotangent_all, activations, preferred_element_ty...  70 us
    ppermute x3, waiting for transfers between devices, _end_targets(): raw_out = lax.ppermute(raw_out, axis_name=chip_axis, perm=block_out)  69.2 us
    unnamed x23, local copies, waits for them, and re-layouts  36.2 us
    all_gather x1, waiting for transfers between devices, body(): grad_full = lax.all_gather(grad_blocks, 'solver', axis=2, tiled=True)  33.1 us
    dot_general x1, matrix products, body(): jnp.einsum('bnm,bnk->bmk', grad_full, grad_full, preferred_element_type=j...  15.2 us
  transfers between devices with their start and end apart: 9, of which 7 were waited for; matrix products, arithmetic and copies ran while one was open for 47% of the time, Pallas kernels for 0%

profile of v1, /device:TPU:0, one launch (start us, length us, event | category | flops | bytes accessed | tf_op | source)
XLA Modules:
  0.0 666.3 jit_solution(8559374710516171483)
XLA Ops:
  7.2 0.7 all-gather.6.cloned.1.call-update
  8.0 77.7 %all-gather.6.cloned.1.call-done = bf16[8192,256]{1,0:T(8,128)(2,1)} async-done(((bf16[1024,256]{1,0:T(8,128)(2,1)}), bf16[8192,256]{1,0:T(8,128)(2,1)}) %all-gather.6.cloned.1.call-update) | async-done | bytes 4194320 | tf_op jit(solution)/shard_map/all_gather | solution.py:64
  85.7 7.8 %convolution_convert_fusion = bf16[8192,512]{1,0:T(8,128)(2,1)} fusion(bf16[8192,256]{1,0:T(8,128)(2,1)} %all-gather.6.cloned.1.call-done, bf16[256,512]{1,0:T(8,128)(2,1)S(1)} %copy-done), kind=kOutput, calls=%fused_computation | convolution fusion | flops 2151677952 | bytes 12845056 | tf_op jit(solution)/shard_map/dot_general | solution.py:66
  93.5 70.0 %reduce-scatter.6.cloned.1.call-done = bf16[2048,512]{1,0:T(8,128)(2,1)} async-done(((bf16[8192,512]{1,0:T(8,128)(2,1)}), bf16[2048,512]{1,0:T(8,128)(2,1)}) %reduce-scatter.6.cloned.1.call-update) | async-done | bytes 2097168 | tf_op jit(solution)/shard_map/reduce_scatter | solution.py:65
  163.5 3.9 copy.32
  167.5 0.5 all-gather.4.cloned.1.call-update
  168.1 0.2 reduce-scatter.4.cloned.1.call-start
  168.3 2.5 fusion.14
  170.8 2.5 copy.53
  173.3 9.1 %copy.31 = f32[1,2,1024,1024]{2,3,1,0:T(8,128)} copy(f32[1,2,1024,1024]{3,2,1,0:T(8,128)} %param.8) | data formatting | bytes 16777216 | tf_op args[3]
  182.4 8.7 %copy.35 = f32[1,2,1024,1024]{2,3,1,0:T(8,128)} copy(f32[1,2,1024,1024]{3,2,1,0:T(8,128)} %param.9) | data formatting | bytes 16777216 | tf_op args[4]
  191.3 33.1 %all-gather.8.cloned.1.call-done = bf16[2,1024,1024]{1,2,0:T(8,128)(2,1)} async-done(((bf16[2,1024,512]{1,2,0:T(8,128)(2,1)}), bf16[2,1024,1024]{1,2,0:T(8,128)(2,1)}) %all-gather.8.cloned.1.call-update) | async-done | bytes 4194320 | tf_op jit(solution)/shard_map/all_gather | solution.py:74
  224.4 15.2 %abs_reduce_fusion.1 = (f32[2,1024]{1,0:T(2,128)S(1)}, f32[2,1024,1024]{1,2,0:T(8,128)}) fusion(bf16[2,1024,1024]{1,2,0:T(8,128)(2,1)} %all-gather.8.cloned.1.call-done, f32[1,2,1024,1024]{2,3,1,0:T(8,128)} %copy.31), kind=kOutput, calls=%fused_computation.9 | convolution fusion | flops 4305451008 | bytes 20979712 | tf_op jit(solution)/shard_map/bnm,bnk->bmk/dot_general | solution.py:75
  239.6 10.1 %abs_reduce_fusion = (f32[2,1024]{1,0:T(2,128)S(1)}, f32[2,1024,1024]{1,2,0:T(8,128)}) fusion(bf16[2,1024,1024]{1,2,0:T(8,128)(2,1)S(1)} %copy-done.3, f32[1,2,1024,1024]{2,3,1,0:T(8,128)} %copy.35), kind=kOutput, calls=%fused_computation.7 | convolution fusion | flops 4305451008 | bytes 20979712 | tf_op jit(solution)/shard_map/bnm,bkm->bnk/dot_general | solution.py:76
  249.9 11.4 %subtract_multiply_fusion = (f32[2,1024,1024]{1,2,0:T(8,128)S(1)}, f32[2,1024,1024]{1,2,0:T(8,128)}) fusion(f32[2,1024,1024]{1,2,0:T(8,128)} %get-tuple-element.22, f32[2]{0:T(128)S(1)} %get-tuple-element.16, f32[1024,1024]{0,1:T(8,128)} %fusion.14, f32[2,1024,1024]{1,2,0:T(8,128)} %get-tuple-element.24, f32[2]{0:T(128)S(1)} %get-tuple-element.28), kind=kLoop, calls=%fused_computation.6 | loop fusion | flops 12582912 | bytes 37748752 | tf_op jit(solution)/shard_map/mul | solution.py:43
  261.4 31.4 %fusion.11 = f32[2,512,1024]{2,1,0:T(8,128)S(1)} fusion(f32[2,1024,1024]{1,2,0:T(8,128)} %get-tuple-element.20, s32[]{:T(128)S(6)} %select_n.18), kind=kOutput, calls=%fused_computation.24 | convolution fusion | flops 12884901888 | bytes 16777220 | tf_op jit(solution)/shard_map/bij,bjk->bik/dot_general | solution.py:30
  292.8 14.3 %fusion.24 = f32[2,512,1024]{2,1,0:T(8,128)S(1)} fusion(f32[2,512,1024]{2,1,0:T(8,128)S(1)} %fusion.11, f32[2,1024,1024]{1,2,0:T(8,128)S(1)} %copy-done.1), kind=kOutput, calls=%fused_computation.53 | convolution fusion | flops 12884901888 | bytes 16777216 | tf_op jit(solution)/shard_map/bij,bjk->bik/dot_general | solution.py:30
  307.1 14.3 %fusion.25 = f32[2,512,1024]{2,1,0:T(8,128)S(1)} fusion(f32[2,512,1024]{2,1,0:T(8,128)S(1)} %fusion.24, f32[2,1024,1024]{1,2,0:T(8,128)S(1)} %copy-done.1), kind=kOutput, calls=%fused_computation.54 | convolution fusion | flops 12884901888 | bytes 16777216 | tf_op jit(solution)/shard_map/bij,bjk->bik/dot_general | solution.py:30
  321.4 16.3 %fusion.3 = f32[2,512,1024]{2,1,0:T(8,128)S(1)} fusion(f32[2,512,1024]{2,1,0:T(8,128)S(1)} %fusion.25, f32[2,1024,1024]{1,2,0:T(8,128)} %get-tuple-element.24, f32[2]{0:T(128)S(1)} %get-tuple-element.28), kind=kOutput, calls=%fused_computation.12 | convolution fusion | flops 12886999040 | bytes 16777224 | tf_op jit(solution)/shard_map/bij,bjk->bik/dot_general | solution.py:30
  337.7 15.6 %fusion.8 = f32[2,512,1024]{2,1,0:T(8,128)} fusion(f32[2,1024,1024]{1,2,0:T(8,128)S(1)} %copy-done.1, f32[2,512,1024]{2,1,0:T(8,128)S(1)} %fusion.3, f32[512,1024]{1,0:T(8,128)S(1)} %fusion.18), kind=kOutput, calls=%fused_computation.21 | convolution fusion | flops 12886999040 | bytes 18874368 | tf_op jit(solution)/shard_map/bij,bjk->bik/dot_general | solution.py:30
  353.3 9.4 %fusion.6 = f32[2,512,1024]{2,1,0:T(8,128)S(1)} fusion(bf16[2,1024,1024]{1,2,0:T(8,128)(2,1)} %all-gather.8.cloned.1.call-done, f32[2,512,1024]{2,1,0:T(8,128)} %fusion.8, f32[2]{0:T(128)S(1)} %get-tuple-element.27), kind=kOutput, calls=%fused_computation.19 | convolution fusion | flops 12885950464 | bytes 12582920 | tf_op jit(solution)/shard_map/brm,bnm->brn/dot_general | solution.py:95
  362.7 14.3 %fusion.26 = f32[2,512,1024]{2,1,0:T(8,128)S(1)} fusion(f32[2,512,1024]{2,1,0:T(8,128)S(1)} %fusion.6, f32[2,1024,1024]{1,2,0:T(8,128)S(1)} %get-tuple-element.19), kind=kOutput, calls=%fused_computation.55 | convolution fusion | flops 12884901888 | bytes 16777216 | tf_op jit(solution)/shard_map/bij,bjk->bik/dot_general | solution.py:30
  377.1 14.6 %fusion.27 = f32[2,512,1024]{2,1,0:T(8,128)S(1)} fusion(f32[2,512,1024]{2,1,0:T(8,128)S(1)} %fusion.26, f32[2,1024,1024]{1,2,0:T(8,128)S(1)} %get-tuple-element.19), kind=kOutput, calls=%fused_computation.56 | convolution fusion | flops 12884901888 | bytes 16777216 | tf_op jit(solution)/shard_map/bij,bjk->bik/dot_general | solution.py:30
  391.7 14.3 %fusion.28 = f32[2,512,1024]{2,1,0:T(8,128)S(1)} fusion(f32[2,512,1024]{2,1,0:T(8,128)S(1)} %fusion.27, f32[2,1024,1024]{1,2,0:T(8,128)S(1)} %get-tuple-element.19), kind=kOutput, calls=%fused_computation.57 | convolution fusion | flops 12884901888 | bytes 16777216 | tf_op jit(solution)/shard_map/bij,bjk->bik/dot_general | solution.py:30
  406.0 14.4 %fusion.29 = f32[2,512,1024]{2,1,0:T(8,128)S(1)} fusion(f32[2,512,1024]{2,1,0:T(8,128)S(1)} %fusion.28, f32[2,1024,1024]{1,2,0:T(8,128)S(1)} %get-tuple-element.19), kind=kOutput, calls=%fused_computation.58 | convolution fusion | flops 12884901888 | bytes 16777216 | tf_op jit(solution)/shard_map/bij,bjk->bik/dot_general | solution.py:30
  420.4 14.7 %fusion.30 = f32[2,512,1024]{2,1,0:T(8,128)S(1)} fusion(f32[2,512,1024]{2,1,0:T(8,128)S(1)} %fusion.29, f32[2,1024,1024]{1,2,0:T(8,128)S(1)} %get-tuple-element.19), kind=kOutput, calls=%fused_computation.59 | convolution fusion | flops 12884901888 | bytes 16777216 | tf_op jit(solution)/shard_map/bij,bjk->bik/dot_general | solution.py:30
  435.1 16.0 %multiply_reduce_fusion = (f32[2]{0:T(128)S(1)}, f32[2,512,1024]{2,1,0:T(8,128)}) fusion(f32[2]{0:T(128)S(1)} %get-tuple-element.15, f32[2,512,1024]{2,1,0:T(8,128)S(1)} %fusion.30, f32[2,1024,1024]{1,2,0:T(8,128)S(1)} %bitcast.40, f32[2]{0:T(128)S(1)} %get-tuple-element.16, f32[2,512,1024]{2,1,0:T(8,128)S(1)} %fusion.26), kind=kOutput, calls=%fused_computation.16 | convolution fusion | flops 12892241920 | bytes 20971544 | tf_op jit(solution)/shard_map/bij,bjk->bik/dot_general | solution.py:30
  451.1 4.9 psum.7
  456.0 5.1 divide_bitcast_fusion
  461.1 5.4 copy.52
  466.5 3.5 subtract_convert_fusion
  470.1 7.7 %convolution_convert_fusion.2 = bf16[8192,256]{1,0:T(8,128)(2,1)} fusion(bf16[512,8192]{1,0:T(8,128)(2,1)} %all-gather.4.cloned.1.call-done, bf16[256,512]{1,0:T(8,128)(2,1)S(1)} %copy-done), kind=kOutput, calls=%fused_computation.2 | convolution fusion | flops 2149580800 | bytes 12845056 | tf_op jit(solution)/shard_map/dot_general | solution.py:48
  477.9 17.7 %collective-permute-done = bf16[512,2048]{0,1:T(8,128)(2,1)} collective-permute-done((bf16[512,2048]{0,1:T(8,128)(2,1)S(1)}, bf16[512,2048]{0,1:T(8,128)(2,1)}, u32[]{:S(2)}, u32[]{:S(2)}) %collective-permute-start) | collective-permute-done | bytes 2097184 | tf_op jit(solution)/shard_map/ppermute | solution.py:19
  495.7 25.8 %collective-permute-done.1 = bf16[512,2048]{0,1:T(8,128)(2,1)} collective-permute-done((bf16[512,2048]{0,1:T(8,128)(2,1)}, bf16[512,2048]{0,1:T(8,128)(2,1)}, u32[]{:S(2)}, u32[]{:S(2)}) %collective-permute-start.1) | collective-permute-done | bytes 2097184 | tf_op jit(solution)/shard_map/ppermute | solution.py:19
  521.7 25.7 %collective-permute-done.2 = bf16[512,2048]{0,1:T(8,128)(2,1)} collective-permute-done((bf16[512,2048]{0,1:T(8,128)(2,1)}, bf16[512,2048]{0,1:T(8,128)(2,1)}, u32[]{:S(2)}, u32[]{:S(2)}) %collective-permute-start.2) | collective-permute-done | bytes 2097184 | tf_op jit(solution)/shard_map/ppermute | solution.py:19
  547.4 1.7 constant_dynamic-update-slice_fusion.7
  549.1 1.7 constant_dynamic-update-slice_fusion.6
  550.9 1.7 constant_dynamic-update-slice_fusion.5
  552.7 1.7 constant_dynamic-update-slice_fusion.3
  554.5 1.7 constant_dynamic-update-slice_fusion.2
  556.2 1.7 constant_dynamic-update-slice_fusion.1
  558.1 4.3 convolution_convert_fusion.1
  562.5 4.7 constant_dynamic-slice_fusion.1
  567.1 5.3 copy.34
  572.5 4.6 constant_dynamic-slice_fusion
  577.1 5.7 copy.38
  582.8 5.4 copy.54
  588.2 71.1 %reduce-scatter.8.cloned.1.call-done = bf16[1024,256]{1,0:T(8,128)(2,1)} async-done(((bf16[8192,256]{1,0:T(8,128)(2,1)}), bf16[1024,256]{1,0:T(8,128)(2,1)}) %reduce-scatter.8.cloned.1.call-update) | async-done | bytes 524304 | tf_op jit(solution)/shard_map/reduce_scatter | solution.py:116
  (35 shorter events, 1.3 us)
Async XLA Ops:
  7.2 78.5 %copy-start = (bf16[256,512]{1,0:T(8,128)(2,1)S(1)}, bf16[256,512]{1,0:T(8,128)(2,1)}, u32[]{:S(2)}) copy-start(bf16[256,512]{1,0:T(8,128)(2,1)} %param.5) | copy-start | bytes 786436
  7.2 78.5 %all-gather.6.cloned.1.call-start = ((), (), s32[]{:S(2)}) async-start(), calls=%async_computation.5 | async-start | bytes 4718592 | tf_op jit(solution)/shard_map/all_gather | solution.py:64
  7.9 155.6 %reduce-scatter.6.cloned.1.call-start = ((), (), s32[]{:S(2)}) async-start(), calls=%async_computation.6 | async-start | bytes 10485760 | tf_op jit(solution)/shard_map/reduce_scatter | solution.py:65
  93.5 130.9 %all-gather.8.cloned.1.call-start = ((), (), s32[]{:S(2)}) async-start(), calls=%async_computation.7 | async-start | bytes 6291456 | tf_op jit(solution)/shard_map/all_gather | solution.py:74
  167.4 3.4 copy-start.2
  167.5 302.7 %all-gather.4.cloned.1.call-start = ((), (), s32[]{:S(2)}) async-start(), calls=%async_computation.3 | async-start | bytes 10485760 | tf_op jit(solution)/shard_map/all_gather | solution.py:56
  168.1 420.1 %reduce-scatter.4.cloned.1.call-start = ((), (), s32[]{:S(2)}) async-start(), calls=%async_computation.4 | async-start | bytes 4718592 | tf_op jit(solution)/shard_map/reduce_scatter | solution.py:58
  224.4 15.2 %copy-start.3 = (bf16[2,1024,1024]{1,2,0:T(8,128)(2,1)S(1)}, bf16[2,1024,1024]{1,2,0:T(8,128)(2,1)}, u32[]{:S(2)}) copy-start(bf16[2,1024,1024]{1,2,0:T(8,128)(2,1)} %all-gather.8.cloned.1.call-done) | copy-start | bytes 12582916
  261.4 31.4 %copy-start.1 = (f32[2,1024,1024]{1,2,0:T(8,128)S(1)}, f32[2,1024,1024]{1,2,0:T(8,128)}, u32[]{:S(2)}) copy-start(f32[2,1024,1024]{1,2,0:T(8,128)} %get-tuple-element.20) | copy-start | bytes 25165828
  406.0 29.1 %slice-start = ((s8[8388608]{0:T(1024)(128)(4,1)}), s8[4194304]{0:T(1024)(128)(4,1)S(1)}, s32[]{:S(2)}) async-start(s8[8388608]{0:T(1024)(128)(4,1)} %bitcast.39), calls=%async_computation.9 | async-start | bytes 8388608
  420.4 14.7 %slice-start.1 = ((s8[8388608]{0:T(1024)(128)(4,1)}), s8[4194304]{0:T(1024)(128)(4,1)S(1)}, s32[]{:S(2)}) async-start(s8[8388608]{0:T(1024)(128)(4,1)} %bitcast.39), calls=%async_computation.10 | async-start | bytes 8388608
  470.0 25.6 %collective-permute-start = (bf16[512,2048]{0,1:T(8,128)(2,1)S(1)}, bf16[512,2048]{0,1:T(8,128)(2,1)}, u32[]{:S(2)}, u32[]{:S(2)}) collective-permute-start(bf16[512,2048]{0,1:T(8,128)(2,1)S(1)} %subtract_convert_fusion), channel_id=1, source_target_pairs={{0,8},{8,16},{16,24},{24,0},{1,9},{9,17},{17,25},{25,1},{2,10},{10... | collective-permute-start | bytes 6291464 | tf_op jit(solution)/shard_map/ppermute | solution.py:19
  477.9 181.4 %reduce-scatter.8.cloned.1.call-start = ((), (), s32[]{:S(2)}) async-start(), calls=%async_computation.8 | async-start | bytes 4718592 | tf_op jit(solution)/shard_map/reduce_scatter | solution.py:116
  495.7 25.8 %collective-permute-start.1 = (bf16[512,2048]{0,1:T(8,128)(2,1)}, bf16[512,2048]{0,1:T(8,128)(2,1)}, u32[]{:S(2)}, u32[]{:S(2)}) collective-permute-start(bf16[512,2048]{0,1:T(8,128)(2,1)} %collective-permute-done), channel_id=1, source_target_pairs={{0,8},{8,16},{16,24},{24,0},{1,9},{9,17},{17,25},{25,1},{2,10},{10... | collective-permute-start | bytes 6291464 | tf_op jit(solution)/shard_map/ppermute | solution.py:19
  521.4 26.0 %collective-permute-start.2 = (bf16[512,2048]{0,1:T(8,128)(2,1)}, bf16[512,2048]{0,1:T(8,128)(2,1)}, u32[]{:S(2)}, u32[]{:S(2)}) collective-permute-start(bf16[512,2048]{0,1:T(8,128)(2,1)} %collective-permute-done.1), channel_id=1, source_target_pairs={{0,8},{8,16},{16,24},{24,0},{1,9},{9,17},{17,25},{25,1},{2,10},{10... | collective-permute-start | bytes 6291464 | tf_op jit(solution)/shard_map/ppermute | solution.py:19
Sparse Core Ops, SparseCore 0:
  10.1 75.5 all-gather.5
  93.6 69.8 reduce-scatter.5
  167.6 56.7 all-gather.7
  225.8 58.2 all-gather.3
  478.0 89.1 reduce-scatter.3
  571.3 87.9 reduce-scatter.7
